TPU v7x, 256 devices: a whole 4x4x8 slice. The times are simulated.
256 devices in a mesh: dp: 16 (over x_hi, y, core), seq: 16 (over z, x_lo).
Axes of the slice: x: 4 (x_hi: 2, x_lo: 2; x = x_hi * 2 + x_lo), y: 4, z: 8, core: 2. Of those that a mesh axis runs over, the one named last changes fastest.
Arguments:
- layer_input: bfloat16 [16, 2048, 5120], P('dp', 'seq'), may hold values from -6 to 6
- query_states: bfloat16 [16, 2048, 2560], P('dp', 'seq'), may hold values from -24 to 24
- key_states: bfloat16 [16, 2048, 512], P('dp', 'seq'), may hold values from -6 to 6
- out_grad: bfloat16 [16, 2048, 2560], P('dp', 'seq'), may hold values from -12 to 12
- value_weight: bfloat16 [5120, 512], P('dp'), may hold values from -0.078125 to 0.078125
- segment_ids: int32 [16, 2048], P('dp'), may hold values from 0 to 31, as said below
- pair_split: int32 [16, 32], P('dp'), may hold values from 1 to 2047, as said below
Outputs:
- query_grad: bfloat16 [16, 2048, 2560], P('dp', 'seq')
- key_grad: bfloat16 [16, 2048, 512], P('dp', 'seq')
- input_grad: bfloat16 [16, 2048, 5120], P('dp', 'seq')
- weight_grad: float32 [5120, 512], P('dp', 'seq')
Inputs may be any that keep to these rules, and one draw needn't show every extreme that they name: `segment_ids`: each packed row holds 32 sentence pairs numbered 0 to 31 in order along the row; each pair has 16 to 112 positions, every row has a pair of exactly 112, and the pair lengths of a row can be matched two by two into sums of 128. pair_split[r, s] lies after the first position of pair s and at or before its last position; in every row the first pair's second sentence begins at position 1 and the last pair's at position 2047.
All inputs are finite; a program needn't handle non-finite values.
Results may differ from a plain program's by a relative error of at most 0.0057.
Values may be sent and summed in bfloat16 or wider, within the bound.
A program may use at most 128 MiB of HBM per device.

v0:
```python
import jax
import jax.numpy as jnp
from jax import lax
from jax.sharding import PartitionSpec as P

HD = 128


def with_halo(cells, sides, width):
    for axis, dim in sides:
        count = lax.axis_size(axis)
        ends = count - 1
        head = lax.slice_in_dim(cells, 0, width, axis=dim)
        tail = lax.slice_in_dim(cells, cells.shape[dim] - width, cells.shape[dim], axis=dim)
        cells = jnp.concatenate(
            [
                lax.ppermute(tail, axis, [(i, (i + 1) % count) for i in range(ends)]),
                cells,
                lax.ppermute(head, axis, [((i + 1) % count, i) for i in range(ends)]),
            ],
            axis=dim,
        )
    return cells


def passed_along(array, axis, by):
    count = lax.axis_size(axis)
    pairs = [(i, i + by) for i in range(count) if 0 <= i + by < count]
    return lax.ppermute(array, axis, pairs)


def attend_block(query_rows, key_rows, value_rows, grad_rows, visible):
    rows_here = query_rows.shape[0]
    keys_here = key_rows.shape[0]
    head_count = key_rows.shape[1] // HD
    group_size = query_rows.shape[1] // key_rows.shape[1]
    score_scale = HD ** (-0.5)
    high = lax.Precision.HIGHEST
    query_split = query_rows.reshape(rows_here, head_count, group_size, HD)
    grad_split = grad_rows.reshape(rows_here, head_count, group_size, HD)
    key_split = key_rows.reshape(keys_here, head_count, HD)
    value_split = value_rows.reshape(keys_here, head_count, HD)
    query_parts = []
    key_parts = []
    value_parts = []
    for kv_group in range(head_count):
        query_head = query_split[:, kv_group]
        grad_head = grad_split[:, kv_group]
        key_head = key_split[:, kv_group]
        value_head = value_split[:, kv_group]
        scores = (
            jnp.einsum("qgd,kd->gqk", query_head, key_head, preferred_element_type=jnp.float32)
            * score_scale
        )
        masked = jnp.where(visible[None], scores, -1e30)
        highest = jnp.max(masked, axis=-1, keepdims=True)
        weights = jnp.where(visible[None], jnp.exp(masked - highest), 0.0)
        attention = weights / jnp.sum(weights, axis=-1, keepdims=True)
        attention_low = attention.astype(jnp.bfloat16)
        prob_grad = jnp.einsum(
            "qgd,kd->gqk", grad_head, value_head, preferred_element_type=jnp.float32
        )
        row_delta = jnp.sum(attention * prob_grad, axis=-1, keepdims=True)
        score_grad = attention * (prob_grad - row_delta)
        key_wide = key_head.astype(jnp.float32)
        query_wide = query_head.astype(jnp.float32)
        query_parts.append(
            jnp.einsum("gqk,kd->qgd", score_grad, key_wide, precision=high) * score_scale
        )
        key_parts.append(
            jnp.einsum("gqk,qgd->kd", score_grad, query_wide, precision=high) * score_scale
        )
        value_parts.append(
            jnp.einsum("gqk,qgd->kd", attention_low, grad_head, preferred_element_type=jnp.float32)
        )
    query_grad = jnp.stack(query_parts, axis=1).reshape(rows_here, -1)
    kv_grad = jnp.concatenate(key_parts + value_parts, axis=1)
    return (query_grad, kv_grad)


def local(layer_input, query_states, key_states, out_grad, value_weight, segment_ids, pair_split):
    layer_rows = layer_input[0]
    tok_count = layer_rows.shape[0]
    kv_width = key_states.shape[2]
    row_base = lax.axis_index("seq") * tok_count
    columns = layer_rows
    value_rows = jnp.dot(
        columns,
        lax.all_gather(value_weight, "dp", axis=0, tiled=True),
        preferred_element_type=jnp.float32,
    )
    value_low = value_rows.astype(jnp.bfloat16)
    both_states = jnp.concatenate([key_states[0], value_low], axis=1)
    extended = with_halo(both_states, (("seq", 0),), tok_count)
    key_block = extended[:, :kv_width]
    value_block = extended[:, kv_width:]
    seg_row = segment_ids[0]
    fill_ids = jnp.full((tok_count,), -1, jnp.int32)
    padded_ids = jnp.concatenate([fill_ids, seg_row, fill_ids])
    seg_key = lax.dynamic_slice_in_dim(padded_ids, row_base, tok_count + 2 * tok_count, 0)
    seg_query = lax.dynamic_slice_in_dim(seg_row, row_base, tok_count, 0)
    pair_numbers = jnp.arange(pair_split.shape[1], dtype=jnp.int32)
    split_query = jnp.sum(
        jnp.where(seg_query[:, None] == pair_numbers[None, :], pair_split[0][None, :], 0), axis=1
    )
    pos_query = row_base + jnp.arange(tok_count, dtype=jnp.int32)
    pos_key = row_base - tok_count + jnp.arange(tok_count + 2 * tok_count, dtype=jnp.int32)
    visible = (seg_key[None, :] == seg_query[:, None]) & (
        (pos_key[None, :] <= pos_query[:, None]) | (pos_key[None, :] < split_query[:, None])
    )
    query_grad, kv_grad = attend_block(
        query_states[0], key_block, value_block, out_grad[0], visible
    )
    lower_rim = kv_grad[:tok_count]
    upper_rim = kv_grad[tok_count + tok_count :]
    center = kv_grad[tok_count : tok_count + tok_count]
    from_upper = passed_along(lower_rim, "seq", -1)
    from_lower = passed_along(upper_rim, "seq", 1)
    center = center + from_upper + from_lower
    key_grad = center[:, :kv_width].astype(jnp.bfloat16)
    value_grad = center[:, kv_width:].astype(jnp.bfloat16)
    input_grad = lax.dot_general(
        value_grad,
        lax.all_gather(value_weight, "dp", axis=0, tiled=True),
        (((1,), (1,)), ((), ())),
        preferred_element_type=jnp.float32,
    )
    columns = layer_rows
    own_rows = lax.psum_scatter(
        lax.dot_general(
            columns, value_grad, (((0,), (0,)), ((), ())), preferred_element_type=jnp.float32
        ),
        "dp",
        scatter_dimension=0,
        tiled=True,
    )
    summed = lax.psum_scatter(own_rows, "seq", scatter_dimension=1, tiled=True)
    devices_all = lax.axis_size("dp") * lax.axis_size("seq")
    weight_grad = summed / devices_all
    return (
        query_grad.astype(jnp.bfloat16)[None],
        key_grad[None],
        input_grad.astype(jnp.bfloat16)[None],
        weight_grad,
    )


def solution(mesh):
    return jax.shard_map(
        local,
        mesh=mesh,
        in_specs=(
            P("dp", "seq", None),
            P("dp", "seq", None),
            P("dp", "seq", None),
            P("dp", "seq", None),
            P("dp", None),
            P("dp", None),
            P("dp", None),
        ),
        out_specs=(
            P("dp", "seq", None),
            P("dp", "seq", None),
            P("dp", "seq", None),
            P("dp", "seq"),
        ),
        check_vma=False,
    )
```

profile of v0, /device:TPU:16, one launch (start us, length us, event | category | flops | bytes accessed | tf_op | source)
XLA Modules:
  0.0 368.2 jit_solution(11370934144328889524)
XLA Ops:
  7.2 0.7 all-gather.2.cloned.1.call-update
  8.0 0.7 dynamic-slice_bitcast_fusion
  8.6 0.8 fusion.60
  9.4 0.7 select_reduce_fusion
  10.2 66.7 %all-gather.2.cloned.1.call-done = bf16[5120,512]{1,0:T(8,128)(2,1)} async-done(((bf16[320,512]{1,0:T(8,128)(2,1)}), bf16[5120,512]{1,0:T(8,128)(2,1)}) %all-gather.2.cloned.1.call-update) | async-done | bytes 5242896 | tf_op jit(solution)/shard_map/all_gather | solution.py:89
  76.8 3.3 fusion.36
  80.2 0.7 pad_maximum_fusion.2
  80.9 1.3 collective-permute-start.1
  82.2 5.3 %collective-permute-start = (bf16[128,1024]{1,0:T(8,128)(2,1)}, bf16[128,1024]{1,0:T(8,128)(2,1)}, u32[]{:S(2)}, u32[]{:S(2)}) collective-permute-start(bf16[128,1024]{1,0:T(8,128)(2,1)} %pad_maximum_fusion.2), channel_id=1, source_target_pairs={{0,1},{1,2},{2,3},{3,4},{4,5},{5,6},{6,7},{7,8},{8,9},{9,10},{10,1... | collective-permute-start | bytes 786440 | tf_op jit(solution)/shard_map/ppermute | solution.py:17
  87.5 0.5 iota_add_fusion.1
  88.0 0.3 copy.134
  88.3 1.1 copy.137
  89.4 0.8 or_and_fusion
  90.2 1.4 collective-permute-done.1
  91.6 4.6 %collective-permute-done = bf16[128,1024]{1,0:T(8,128)(2,1)} collective-permute-done((bf16[128,1024]{1,0:T(8,128)(2,1)}, bf16[128,1024]{1,0:T(8,128)(2,1)}, u32[]{:S(2)}, u32[]{:S(2)}) %collective-permute-start) | collective-permute-done | bytes 262176 | tf_op jit(solution)/shard_map/ppermute | solution.py:17
  96.2 1.1 pad_maximum_fusion
  97.6 1.4 fusion.76
  98.9 0.6 fusion.75
  99.5 1.4 fusion.80
  101.0 1.4 fusion.79
  102.4 1.4 fusion.78
  103.8 1.4 fusion.77
  105.3 1.6 multiply_reduce_fusion.3
  107.0 0.8 fusion.46
  107.9 0.5 copy-done.3
  108.4 0.3 copy-done.21
  108.7 0.3 multiply_reduce_fusion.2
  109.1 0.7 fusion.44
  109.8 0.2 copy-done.23
  110.0 0.2 copy-done.14
  110.2 0.5 copy-done.19
  110.7 0.3 multiply_reduce_fusion.1
  111.0 0.7 fusion.42
  111.8 0.2 copy-done.24
  112.0 0.2 copy-done.13
  112.2 0.5 copy-done.17
  112.7 0.3 multiply_reduce_fusion
  113.0 0.9 copy-done.26
  113.9 0.8 fusion.40
  114.7 1.8 fusion.35
  116.5 1.8 fusion.34
  118.3 1.8 fusion.33
  120.1 1.8 fusion.32
  122.0 1.3 collective-permute-start.2
  123.3 5.2 %collective-permute-start.3 = (f32[128,1024]{0,1:T(8,128)S(1)}, f32[128,1024]{0,1:T(8,128)S(1)}, u32[]{:S(2)}, u32[]{:S(2)}) collective-permute-start(f32[128,1024]{0,1:T(8,128)S(1)} %get-tuple-element.21), channel_id=1, source_target_pairs={{0,1},{1,2},{2,3},{3,4},{4,5},{5,6},{6,7},{7,8},{8,9},{9,10},{10,1... | collective-permute-start | bytes 1572872 | tf_op jit(solution)/shard_map/ppermute | solution.py:29
  128.5 9.9 %collective-permute-done.2 = f32[128,1024]{0,1:T(8,128)S(1)} collective-permute-done((f32[128,1024]{0,1:T(8,128)S(1)}, f32[128,1024]{0,1:T(8,128)S(1)}, u32[]{:S(2)}, u32[]{:S(2)}) %collective-permute-start.2) | collective-permute-done | bytes 524320 | tf_op jit(solution)/shard_map/ppermute | solution.py:29
  138.5 11.4 %collective-permute-done.3 = f32[128,1024]{0,1:T(8,128)S(1)} collective-permute-done((f32[128,1024]{0,1:T(8,128)S(1)}, f32[128,1024]{0,1:T(8,128)S(1)}, u32[]{:S(2)}, u32[]{:S(2)}) %collective-permute-start.3) | collective-permute-done | bytes 524320 | tf_op jit(solution)/shard_map/ppermute | solution.py:29
  149.9 5.3 %convolution_bitcast_fusion = f32[5120,512]{0,1:T(8,128)} fusion(bf16[1,128,5120]{2,1,0:T(8,128)(2,1)S(1)} %copy-done, bf16[128,1024]{0,1:T(8,128)(2,1)S(1)} %fusion.52), kind=kOutput, calls=%fused_computation.4 | convolution fusion | flops 671088640 | bytes 11927552 | tf_op jit(solution)/shard_map/dot_general | solution.py:130
  155.3 11.4 %copy.205 = f32[5120,512]{1,0:T(8,128)} copy(f32[5120,512]{0,1:T(8,128)} %convolution_bitcast_fusion) | data formatting | bytes 20971520
  166.7 0.8 copy-done.12
  167.6 2.2 fusion.50
  169.8 116.5 %reduce-scatter.7.cloned.1.call-done = f32[320,512]{1,0:T(8,128)} async-done(((f32[5120,512]{1,0:T(8,128)}), f32[320,512]{1,0:T(8,128)}) %reduce-scatter.7.cloned.1.call-update) | async-done | bytes 655376
  286.2 2.2 copy.206
  288.6 2.3 fusion.49
  291.0 0.7 fusion.48
  291.7 0.2 copy-done.6
  291.9 0.4 copy-done.18
  292.3 0.3 copy-done.27
  292.6 0.7 fusion.47
  293.3 1.1 copy.175
  294.4 0.8 copy.176
  295.2 5.4 %fusion.4 = bf16[1,128,5120]{2,1,0:T(8,128)(2,1)} fusion(bf16[5120,512]{1,0:T(8,128)(2,1)} %all-gather.2.cloned.1.call-done, bf16[128,1024]{0,1:T(8,128)(2,1)S(1)} %fusion.52), kind=kOutput, calls=%fused_computation.6 | convolution fusion | flops 671744000 | bytes 6684672 | tf_op jit(solution)/shard_map/dot_general | solution.py:122
  300.6 59.7 %reduce-scatter.5.cloned.1.call-done = f32[320,32]{0,1:T(8,128)} async-done(((f32[320,512]{0,1:T(8,128)}), f32[320,32]{0,1:T(8,128)}) %reduce-scatter.5.cloned.1.call-update) | async-done | bytes 40976 | tf_op jit(solution)/shard_map/reduce_scatter | solution.py:137
  360.3 1.4 broadcast_multiply_fusion
  (74 shorter events, 1.0 us)
Async XLA Ops:
  7.2 69.7 %copy-start = (bf16[1,128,5120]{2,1,0:T(8,128)(2,1)S(1)}, bf16[1,128,5120]{2,1,0:T(8,128)(2,1)}, u32[]{:S(2)}) copy-start(bf16[1,128,5120]{2,1,0:T(8,128)(2,1)} %param.7) | copy-start | bytes 3932164
  7.2 69.6 %all-gather.2.cloned.1.call-start = ((), (), s32[]{:S(2)}) async-start(), calls=%async_computation.2 | async-start | bytes 5570560 | tf_op jit(solution)/shard_map/all_gather | solution.py:89
  7.9 278.3 %reduce-scatter.7.cloned.1.call-start = ((), (), s32[]{:S(2)}) async-start(), calls=%async_computation.4 | async-start | bytes 11141120
  10.2 70.0 %copy-start.4 = (bf16[1,128,512]{2,1,0:T(8,128)(2,1)S(1)}, bf16[1,128,512]{2,1,0:T(8,128)(2,1)}, u32[]{:S(2)}) copy-start(bf16[1,128,512]{2,1,0:T(8,128)(2,1)} %param.9) | copy-start | bytes 393220
  10.2 77.8 %copy-start.1 = (bf16[1,128,2560]{2,1,0:T(8,128)(2,1)S(1)}, bf16[1,128,2560]{2,1,0:T(8,128)(2,1)}, u32[]{:S(2)}) copy-start(bf16[1,128,2560]{2,1,0:T(8,128)(2,1)} %param.8) | copy-start | bytes 1966084
  80.2 8.1 %copy-start.2 = (bf16[1,128,2560]{2,1,0:T(8,128)(2,1)S(1)}, bf16[1,128,2560]{2,1,0:T(8,128)(2,1)}, u32[]{:S(2)}) copy-start(bf16[1,128,2560]{2,1,0:T(8,128)(2,1)} %param.10) | copy-start | bytes 1966084
  80.9 10.7 %collective-permute-start.1 = (bf16[128,1024]{1,0:T(8,128)(2,1)}, bf16[128,1024]{1,0:T(8,128)(2,1)}, u32[]{:S(2)}, u32[]{:S(2)}) collective-permute-start(bf16[128,1024]{1,0:T(8,128)(2,1)} %pad_maximum_fusion.2), channel_id=1, source_target_pairs={{1,0},{2,1},{3,2},{4,3},{5,4},{6,5},{7,6},{8,7},{9,8},{10,9},{11,1... | collective-permute-start | bytes 786440 | tf_op jit(solution)/shard_map/ppermute | solution.py:19
  82.2 14.0 %collective-permute-start = (bf16[128,1024]{1,0:T(8,128)(2,1)}, bf16[128,1024]{1,0:T(8,128)(2,1)}, u32[]{:S(2)}, u32[]{:S(2)}) collective-permute-start(bf16[128,1024]{1,0:T(8,128)(2,1)} %pad_maximum_fusion.2), channel_id=1, source_target_pairs={{0,1},{1,2},{2,3},{3,4},{4,5},{5,6},{6,7},{7,8},{8,9},{9,10},{10,1... | collective-permute-start | bytes 786440 | tf_op jit(solution)/shard_map/ppermute | solution.py:17
  90.2 13.6 %copy-start.16 = (pred[128,384]{0,1:T(8,128)(4,1)}, pred[128,384]{0,1:T(8,128)(4,1)S(1)}, u32[]{:S(2)}) copy-start(pred[128,384]{0,1:T(8,128)(4,1)S(1)} %or_and_fusion) | copy-start | bytes 147460
  99.5 2.9 copy-start.9
  99.5 2.9 copy-start.11
  99.5 2.9 copy-start.7
  99.5 4.3 %copy-start.5 = (bf16[384,1,128]{2,1,0:T(2,128)(2,1)}, bf16[384,1,128]{2,1,0:T(2,128)(2,1)S(1)}, u32[]{:S(2)}) copy-start(bf16[384,1,128]{2,1,0:T(2,128)(2,1)S(1)} %get-tuple-element.27) | copy-start | bytes 294916
  105.3 1.7 copy-start.22
  106.9 1.0 copy-start.28
  106.9 1.0 copy-start.35
  106.9 1.4 copy-start.3
  107.0 1.5 copy-start.15
  107.0 1.8 copy-start.21
  109.0 1.0 copy-start.23
  109.0 1.0 copy-start.29
  109.1 1.2 copy-start.14
  109.1 1.6 copy-start.19
  111.0 1.0 copy-start.24
  111.0 1.0 copy-start.31
  111.0 1.2 copy-start.13
  111.0 1.6 copy-start.17
  113.0 0.9 copy-start.26
  113.0 0.9 copy-start.33
  122.0 16.5 %collective-permute-start.2 = (f32[128,1024]{0,1:T(8,128)S(1)}, f32[128,1024]{0,1:T(8,128)S(1)}, u32[]{:S(2)}, u32[]{:S(2)}) collective-permute-start(f32[128,1024]{0,1:T(8,128)S(1)} %get-tuple-element.20), channel_id=1, source_target_pairs={{1,0},{2,1},{3,2},{4,3},{5,4},{6,5},{7,6},{8,7},{9,8},{10,9},{11,1... | collective-permute-start | bytes 1572872 | tf_op jit(solution)/shard_map/ppermute | solution.py:29
  123.3 26.6 %collective-permute-start.3 = (f32[128,1024]{0,1:T(8,128)S(1)}, f32[128,1024]{0,1:T(8,128)S(1)}, u32[]{:S(2)}, u32[]{:S(2)}) collective-permute-start(f32[128,1024]{0,1:T(8,128)S(1)} %get-tuple-element.21), channel_id=1, source_target_pairs={{0,1},{1,2},{2,3},{3,4},{4,5},{5,6},{6,7},{7,8},{8,9},{9,10},{10,1... | collective-permute-start | bytes 1572872 | tf_op jit(solution)/shard_map/ppermute | solution.py:29
  166.6 0.9 copy-start.12
  166.6 0.9 copy-start.36
  166.7 193.6 %reduce-scatter.5.cloned.1.call-start = ((), (), s32[]{:S(2)}) async-start(), calls=%async_computation.3 | async-start | bytes 835584 | tf_op jit(solution)/shard_map/reduce_scatter | solution.py:137
  169.7 118.8 %copy-start.10 = (bf16[384,1,128]{2,1,0:T(2,128)(2,1)S(1)}, bf16[384,1,128]{2,1,0:T(2,128)(2,1)}, u32[]{:S(2)}) copy-start(bf16[384,1,128]{2,1,0:T(2,128)(2,1)} %copy-done.9) | copy-start | bytes 294916
  169.8 118.8 %copy-start.30 = (f32[5,128]{1,0:T(8,128)S(1)}, f32[5,128]{1,0:T(8,128)}, u32[]{:S(2)}) copy-start(f32[5,128]{1,0:T(8,128)} %copy-done.29) | copy-start | bytes 7684
  288.5 2.4 copy-start.8
  288.5 2.4 copy-start.20
  288.6 2.4 copy-start.25
  288.6 2.4 copy-start.32
  290.9 0.9 copy-start.6
  291.0 1.3 copy-start.18
  291.0 1.6 copy-start.27
  291.0 1.6 copy-start.34
Sparse Core Ops, SparseCore 0:
  10.8 65.9 all-gather.1
  166.8 119.4 reduce-scatter.6
  288.8 71.4 reduce-scatter.4
where the time goes:
time: 369 us; the launch traced here: 368 us
  waiting for transfers between devices  271 us (73%)
  matrix products  38.3 us (10%)
  local copies, waits for them, and re-layouts  25.4 us (7%)
  between operations  14.3 us (4%)
  starting transfers between devices  13.2 us (4%)
  other arithmetic  6.26 us (2%)
    unnamed x4, waiting for transfers between devices  117 us
    all_gather x1, waiting for transfers between devices, local(): lax.all_gather(value_weight, 'dp', axis=0, tiled=True)  66.7 us
    reduce_scatter x1, waiting for transfers between devices, local(): summed = lax.psum_scatter(own_rows, 'seq', scatter_dimension=1, tiled=True)  59.7 us
    unnamed x80, local copies, waits for them, and re-layouts  22.4 us
    ppermute x2, waiting for transfers between devices, passed_along(): return lax.ppermute(array, axis, pairs)  21.3 us
  transfers between devices with their start and end apart: 7, of which 7 were waited for; matrix products, arithmetic and copies ran while one was open for 5% of the time, Pallas kernels for 0%

commit v1 on v0

--- a/solution.py
+++ b/solution.py
@@ -86,7 +86,9 @@
     columns = layer_rows
     value_rows = jnp.dot(
         columns,
-        lax.all_gather(value_weight, "dp", axis=0, tiled=True),
+        jnp.concatenate(
+            lax.all_to_all(jnp.stack([value_weight] * lax.axis_size("dp")), "dp", 0, 0), axis=0
+        ),
         preferred_element_type=jnp.float32,
     )
     value_low = value_rows.astype(jnp.bfloat16)

time: 369 us -> 456 us (1.24)
  waiting for transfers between devices: 271 us -> 348 us
  starting transfers between devices: 13.2 us -> 21.4 us
    all_to_all x0 -> x1, waiting for transfers between devices: none -> 67 us  [local(): lax.all_to_all(jnp.stack([value_weight] * lax.axis_size('dp')), 'dp', 0, 0)]
    unnamed x4, waiting for transfers between devices: 117 us -> 127 us
    all_gather x1, waiting for transfers between devices: 66.7 us -> 57.4 us  [local(): lax.all_gather(value_weight, 'dp', axis=0, tiled=True)]
    reduce_scatter x1, waiting for transfers between devices: 59.7 us -> 67.6 us  [local(): summed = lax.psum_scatter(own_rows, 'seq', scatter_dimension=1, tiled=True)]
    all_to_all x0 -> x1, starting transfers between devices: none -> 7.41 us  [local(): lax.all_to_all(jnp.stack([value_weight] * lax.axis_size('dp')), 'dp', 0, 0)]
    unnamed x80 -> x90, local copies, waits for them, and re-layouts: 22.4 us -> 22 us
  transfers between devices with their start and end apart: 7 -> 8, of which waited for: 7 -> 8; matrix products, arithmetic and copies ran while one was open for 5% -> 4% of each run, Pallas kernels for 0% -> 0%
where the time goes in v1:
time: 456 us; the launch traced here: 455 us
  waiting for transfers between devices  348 us (76%)
  matrix products  38.2 us (8%)
  local copies, waits for them, and re-layouts  28.2 us (6%)
  starting transfers between devices  21.4 us (5%)
  between operations  14.3 us (3%)
  other arithmetic  4.92 us (1%)
    unnamed x4, waiting for transfers between devices  127 us
    reduce_scatter x1, waiting for transfers between devices, local(): summed = lax.psum_scatter(own_rows, 'seq', scatter_dimension=1, tiled=True)  67.6 us
    all_to_all x1, waiting for transfers between devices, local(): lax.all_to_all(jnp.stack([value_weight] * lax.axis_size('dp')), 'dp', 0, 0)  67 us
    all_gather x1, waiting for transfers between devices, local(): lax.all_gather(value_weight, 'dp', axis=0, tiled=True)  57.4 us
    unnamed x90, local copies, waits for them, and re-layouts  22 us
    ppermute x2, waiting for transfers between devices, passed_along(): return lax.ppermute(array, axis, pairs)  21.4 us
  transfers between devices with their start and end apart: 8, of which 8 were waited for; matrix products, arithmetic and copies ran while one was open for 4% of the time, Pallas kernels for 0%

profile of v1, /device:TPU:16, one launch (start us, length us, event | category | flops | bytes accessed | tf_op | source)
XLA Modules:
  0.0 455.3 jit_solution(14181386477449865617)
XLA Ops:
  7.2 3.9 stack.17
  11.1 7.4 %all-to-all-start = ((bf16[16,320,512]{2,1,0:T(8,128)(2,1)}), bf16[16,320,512]{2,1,0:T(8,128)(2,1)}, u32[]{:S(2)}, u32[]{:S(2)}) async-start(bf16[16,320,512]{2,1,0:T(8,128)(2,1)} %stack.17), calls=%async_computation | async-start | bytes 10485760 | tf_op jit(solution)/shard_map/all_to_all | solution.py:90
  18.8 67.0 %all-to-all-done = bf16[16,320,512]{2,1,0:T(8,128)(2,1)} async-done(((bf16[16,320,512]{2,1,0:T(8,128)(2,1)}), bf16[16,320,512]{2,1,0:T(8,128)(2,1)}, u32[]{:S(2)}, u32[]{:S(2)}) %all-to-all-start) | async-done | bytes 5242912 | tf_op jit(solution)/shard_map/all_to_all | solution.py:90
  85.8 3.4 fusion.36
  89.3 0.7 pad_maximum_fusion.2
  90.0 1.3 collective-permute-start.1
  91.3 6.1 %collective-permute-start = (bf16[128,1024]{1,0:T(8,128)(2,1)}, bf16[128,1024]{1,0:T(8,128)(2,1)}, u32[]{:S(2)}, u32[]{:S(2)}) collective-permute-start(bf16[128,1024]{1,0:T(8,128)(2,1)} %pad_maximum_fusion.2), channel_id=1, source_target_pairs={{0,1},{1,2},{2,3},{3,4},{4,5},{5,6},{6,7},{7,8},{8,9},{9,10},{10,1... | collective-permute-start | bytes 786440 | tf_op jit(solution)/shard_map/ppermute | solution.py:17
  97.4 0.5 iota_add_fusion.1
  97.9 0.3 copy.134
  98.3 1.1 copy.137
  99.3 0.8 or_and_fusion
  100.2 2.0 collective-permute-done.1
  102.2 5.8 %collective-permute-done = bf16[128,1024]{1,0:T(8,128)(2,1)} collective-permute-done((bf16[128,1024]{1,0:T(8,128)(2,1)}, bf16[128,1024]{1,0:T(8,128)(2,1)}, u32[]{:S(2)}, u32[]{:S(2)}) %collective-permute-start) | collective-permute-done | bytes 262176 | tf_op jit(solution)/shard_map/ppermute | solution.py:17
  108.0 1.1 pad_maximum_fusion
  109.4 1.4 fusion.76
  110.8 0.6 fusion.75
  111.4 1.4 fusion.80
  112.8 1.5 fusion.78
  114.3 1.4 fusion.79
  115.7 1.4 fusion.77
  117.1 1.3 multiply_reduce_fusion.3
  118.5 0.1 copy-done.27
  118.6 0.8 fusion.46
  119.4 0.5 copy-done.5
  120.0 0.3 copy-done.25
  120.3 0.3 multiply_reduce_fusion.1
  120.6 0.6 copy-done.16
  121.2 0.6 copy-done.23
  121.8 0.3 multiply_reduce_fusion.2
  122.1 0.8 fusion.44
  122.9 0.3 copy-done.28
  123.1 0.8 fusion.42
  123.9 0.2 copy-done.15
  124.1 0.4 copy-done.21
  124.4 0.3 multiply_reduce_fusion
  124.8 0.9 copy-done.31
  125.7 0.8 fusion.40
  126.5 1.9 fusion.35
  128.4 1.8 fusion.34
  130.2 1.8 fusion.33
  132.0 1.8 fusion.32
  133.9 1.3 collective-permute-start.2
  135.2 5.2 %collective-permute-start.3 = (f32[128,1024]{0,1:T(8,128)S(1)}, f32[128,1024]{0,1:T(8,128)S(1)}, u32[]{:S(2)}, u32[]{:S(2)}) collective-permute-start(f32[128,1024]{0,1:T(8,128)S(1)} %get-tuple-element.21), channel_id=1, source_target_pairs={{0,1},{1,2},{2,3},{3,4},{4,5},{5,6},{6,7},{7,8},{8,9},{9,10},{10,1... | collective-permute-start | bytes 1572872 | tf_op jit(solution)/shard_map/ppermute | solution.py:29
  140.5 10.0 %collective-permute-done.2 = f32[128,1024]{0,1:T(8,128)S(1)} collective-permute-done((f32[128,1024]{0,1:T(8,128)S(1)}, f32[128,1024]{0,1:T(8,128)S(1)}, u32[]{:S(2)}, u32[]{:S(2)}) %collective-permute-start.2) | collective-permute-done | bytes 524320 | tf_op jit(solution)/shard_map/ppermute | solution.py:29
  150.5 11.4 %collective-permute-done.3 = f32[128,1024]{0,1:T(8,128)S(1)} collective-permute-done((f32[128,1024]{0,1:T(8,128)S(1)}, f32[128,1024]{0,1:T(8,128)S(1)}, u32[]{:S(2)}, u32[]{:S(2)}) %collective-permute-start.3) | collective-permute-done | bytes 524320 | tf_op jit(solution)/shard_map/ppermute | solution.py:29
  161.9 5.3 %convolution_bitcast_fusion = f32[5120,512]{0,1:T(8,128)} fusion(bf16[1,128,5120]{2,1,0:T(8,128)(2,1)S(1)} %copy-done, bf16[128,1024]{0,1:T(8,128)(2,1)S(1)} %fusion.52), kind=kOutput, calls=%fused_computation.4 | convolution fusion | flops 671088640 | bytes 11927552 | tf_op jit(solution)/shard_map/dot_general | solution.py:132
  167.3 11.4 %copy.205 = f32[5120,512]{1,0:T(8,128)} copy(f32[5120,512]{0,1:T(8,128)} %convolution_bitcast_fusion) | data formatting | bytes 20971520
  178.7 0.7 all-gather.2.cloned.1.call-update
  179.5 0.1 copy-done.14
  179.6 2.2 fusion.50
  181.8 126.3 %reduce-scatter.7.cloned.1.call-done = f32[320,512]{1,0:T(8,128)} async-done(((f32[5120,512]{1,0:T(8,128)}), f32[320,512]{1,0:T(8,128)}) %reduce-scatter.7.cloned.1.call-update) | async-done | bytes 655376
  308.0 2.3 copy.206
  310.4 2.3 fusion.48
  312.8 0.7 fusion.49
  313.4 0.2 copy-done.8
  313.6 0.4 copy-done.22
  314.0 0.3 copy-done.32
  314.3 0.7 fusion.47
  315.1 1.1 copy.175
  316.2 0.8 copy.176
  317.0 57.4 %all-gather.2.cloned.1.call-done = bf16[5120,512]{1,0:T(8,128)(2,1)} async-done(((bf16[320,512]{1,0:T(8,128)(2,1)}), bf16[5120,512]{1,0:T(8,128)(2,1)}) %all-gather.2.cloned.1.call-update) | async-done | bytes 5242896 | tf_op jit(solution)/shard_map/all_gather | solution.py:126
  374.4 5.4 %fusion.4 = bf16[1,128,5120]{2,1,0:T(8,128)(2,1)} fusion(bf16[5120,512]{1,0:T(8,128)(2,1)} %all-gather.2.cloned.1.call-done, bf16[128,1024]{0,1:T(8,128)(2,1)S(1)} %fusion.52), kind=kOutput, calls=%fused_computation.6 | convolution fusion | flops 671744000 | bytes 6684672 | tf_op jit(solution)/shard_map/dot_general | solution.py:124
  379.8 67.6 %reduce-scatter.5.cloned.1.call-done = f32[320,32]{0,1:T(8,128)} async-done(((f32[320,512]{0,1:T(8,128)}), f32[320,32]{0,1:T(8,128)}) %reduce-scatter.5.cloned.1.call-update) | async-done | bytes 40976 | tf_op jit(solution)/shard_map/reduce_scatter | solution.py:139
  447.4 1.4 broadcast_multiply_fusion
  (87 shorter events, 1.0 us)
Async XLA Ops:
  7.2 78.7 %copy-start = (bf16[1,128,5120]{2,1,0:T(8,128)(2,1)S(1)}, bf16[1,128,5120]{2,1,0:T(8,128)(2,1)}, u32[]{:S(2)}) copy-start(bf16[1,128,5120]{2,1,0:T(8,128)(2,1)} %param.7) | copy-start | bytes 3932164
  11.1 7.5 %copy-start.19 = (s32[1,2048]{1,0:T(1,128)S(1)}, s32[1,2048]{1,0:T(1,128)}, u32[]{:S(2)}) copy-start(s32[1,2048]{1,0:T(1,128)} %param.12) | copy-start | bytes 24580
  11.1 7.6 %copy-start.20 = (s32[1,32]{1,0:T(1,128)S(1)}, s32[1,32]{1,0:T(1,128)}, u32[]{:S(2)}) copy-start(s32[1,32]{1,0:T(1,128)} %param.13) | copy-start | bytes 388
  11.1 74.7 %all-to-all-start = ((bf16[16,320,512]{2,1,0:T(8,128)(2,1)}), bf16[16,320,512]{2,1,0:T(8,128)(2,1)}, u32[]{:S(2)}, u32[]{:S(2)}) async-start(bf16[16,320,512]{2,1,0:T(8,128)(2,1)} %stack.17), calls=%async_computation | async-start | bytes 10485760 | tf_op jit(solution)/shard_map/all_to_all | solution.py:90
  18.5 289.5 %reduce-scatter.7.cloned.1.call-start = ((), (), s32[]{:S(2)}) async-start(), calls=%async_computation.5 | async-start | bytes 11141120
  85.8 3.4 copy-start.6
  85.8 12.1 %copy-start.1 = (bf16[1,128,2560]{2,1,0:T(8,128)(2,1)S(1)}, bf16[1,128,2560]{2,1,0:T(8,128)(2,1)}, u32[]{:S(2)}) copy-start(bf16[1,128,2560]{2,1,0:T(8,128)(2,1)} %param.8) | copy-start | bytes 1966084
  89.2 9.0 %copy-start.2 = (bf16[1,128,2560]{2,1,0:T(8,128)(2,1)S(1)}, bf16[1,128,2560]{2,1,0:T(8,128)(2,1)}, u32[]{:S(2)}) copy-start(bf16[1,128,2560]{2,1,0:T(8,128)(2,1)} %param.10) | copy-start | bytes 1966084
  90.0 12.2 %collective-permute-start.1 = (bf16[128,1024]{1,0:T(8,128)(2,1)}, bf16[128,1024]{1,0:T(8,128)(2,1)}, u32[]{:S(2)}, u32[]{:S(2)}) collective-permute-start(bf16[128,1024]{1,0:T(8,128)(2,1)} %pad_maximum_fusion.2), channel_id=1, source_target_pairs={{1,0},{2,1},{3,2},{4,3},{5,4},{6,5},{7,6},{8,7},{9,8},{10,9},{11,1... | collective-permute-start | bytes 786440 | tf_op jit(solution)/shard_map/ppermute | solution.py:19
  91.3 16.7 %collective-permute-start = (bf16[128,1024]{1,0:T(8,128)(2,1)}, bf16[128,1024]{1,0:T(8,128)(2,1)}, u32[]{:S(2)}, u32[]{:S(2)}) collective-permute-start(bf16[128,1024]{1,0:T(8,128)(2,1)} %pad_maximum_fusion.2), channel_id=1, source_target_pairs={{0,1},{1,2},{2,3},{3,4},{4,5},{5,6},{6,7},{7,8},{8,9},{9,10},{10,1... | collective-permute-start | bytes 786440 | tf_op jit(solution)/shard_map/ppermute | solution.py:17
  98.2 17.5 %copy-start.3 = (bf16[1,128,2560]{1,2,0:T(8,128)(2,1)}, bf16[1,128,2560]{1,2,0:T(8,128)(2,1)S(1)}, u32[]{:S(2)}) copy-start(bf16[1,128,2560]{1,2,0:T(8,128)(2,1)S(1)} %copy.134) | copy-start | bytes 1966084
  100.2 15.5 %copy-start.18 = (pred[128,384]{0,1:T(8,128)(4,1)}, pred[128,384]{0,1:T(8,128)(4,1)S(1)}, u32[]{:S(2)}) copy-start(pred[128,384]{0,1:T(8,128)(4,1)S(1)} %or_and_fusion) | copy-start | bytes 147460
  111.3 2.9 copy-start.11
  111.4 2.9 copy-start.13
  111.4 2.9 copy-start.9
  111.4 20.7 %copy-start.7 = (bf16[384,1,128]{2,1,0:T(2,128)(2,1)}, bf16[384,1,128]{2,1,0:T(2,128)(2,1)S(1)}, u32[]{:S(2)}) copy-start(bf16[384,1,128]{2,1,0:T(2,128)(2,1)S(1)} %get-tuple-element.27) | copy-start | bytes 294916
  115.7 1.4 copy-start.26
  117.1 1.4 copy-start.4
  117.1 1.5 copy-start.27
  118.5 0.9 copy-start.33
  118.5 0.9 copy-start.40
  118.6 1.3 copy-start.5
  118.6 1.3 copy-start.17
  118.6 1.7 copy-start.25
  120.3 0.9 copy-start.16
  120.3 1.5 copy-start.23
  120.6 2.5 copy-start.30
  120.6 2.5 copy-start.36
  122.1 1.0 copy-start.28
  122.1 1.0 copy-start.34
  123.1 0.9 copy-start.15
  123.1 1.3 copy-start.21
  124.7 0.9 copy-start.31
  124.7 1.7 copy-start.38
  126.5 1.9 copy-start.10
  128.4 1.8 copy-start.12
  133.9 16.6 %collective-permute-start.2 = (f32[128,1024]{0,1:T(8,128)S(1)}, f32[128,1024]{0,1:T(8,128)S(1)}, u32[]{:S(2)}, u32[]{:S(2)}) collective-permute-start(f32[128,1024]{0,1:T(8,128)S(1)} %get-tuple-element.20), channel_id=1, source_target_pairs={{1,0},{2,1},{3,2},{4,3},{5,4},{6,5},{7,6},{8,7},{9,8},{10,9},{11,1... | collective-permute-start | bytes 1572872 | tf_op jit(solution)/shard_map/ppermute | solution.py:29
  135.2 26.6 %collective-permute-start.3 = (f32[128,1024]{0,1:T(8,128)S(1)}, f32[128,1024]{0,1:T(8,128)S(1)}, u32[]{:S(2)}, u32[]{:S(2)}) collective-permute-start(f32[128,1024]{0,1:T(8,128)S(1)} %get-tuple-element.21), channel_id=1, source_target_pairs={{0,1},{1,2},{2,3},{3,4},{4,5},{5,6},{6,7},{7,8},{8,9},{9,10},{10,1... | collective-permute-start | bytes 1572872 | tf_op jit(solution)/shard_map/ppermute | solution.py:29
  178.7 0.9 copy-start.14
  178.7 0.9 copy-start.41
  178.7 195.7 %all-gather.2.cloned.1.call-start = ((), (), s32[]{:S(2)}) async-start(), calls=%async_computation.3 | async-start | bytes 5570560 | tf_op jit(solution)/shard_map/all_gather | solution.py:126
  179.4 267.9 %reduce-scatter.5.cloned.1.call-start = ((), (), s32[]{:S(2)}) async-start(), calls=%async_computation.4 | async-start | bytes 835584 | tf_op jit(solution)/shard_map/reduce_scatter | solution.py:139
  181.8 128.6 %copy-start.37 = (f32[5,128]{1,0:T(8,128)S(1)}, f32[5,128]{1,0:T(8,128)}, u32[]{:S(2)}) copy-start(f32[5,128]{1,0:T(8,128)} %copy-done.36) | copy-start | bytes 7684
  310.3 2.3 copy-start.24
  310.3 2.3 copy-start.29
  310.4 2.3 copy-start.35
  312.7 0.9 copy-start.8
  312.7 1.3 copy-start.22
  312.7 1.6 copy-start.32
  312.7 1.6 copy-start.39
Sparse Core Ops, SparseCore 0:
  178.8 129.1 reduce-scatter.6
  310.8 63.5 all-gather.1
  376.9 70.4 reduce-scatter.4
